TPU v7x, 32 devices: a whole 2x2x4 slice. The times are simulated.
32 devices in a mesh: seq: 4 (over y, x), head: 8 (over z, core).
Axes of the slice: x: 2, y: 2, z: 4, core: 2. Of those that a mesh axis runs over, the one named last changes fastest.
Arguments:
- inputs: bfloat16 [4096, 6144], P('seq', 'head'), may hold values from -6 to 6
- projection: bfloat16 [6144, 3, 4096], P('seq', None, 'head'), may hold values from -0.078125 to 0.078125
- cotangent: bfloat16 [4096, 4096], P('seq', 'head'), may hold values from -0.3125 to 0.3125
- log_decay: float32 [32, 4096], P('head', 'seq'), may hold values from -0.7 to 0
- document_starts: int32 [4], replicated, may hold values from 0 to 3328, as said below
Outputs:
- input_gradient: bfloat16 [4096, 6144], P('seq', 'head')
- weight_gradient: bfloat16 [6144, 3, 4096], P('seq', None, 'head')
Inputs may be any that keep to these rules, and one draw needn't show every extreme that they name: `document_starts`: strictly increasing; the first is 0 and the last is (3) * 1024 + 256.
All inputs are finite; a program needn't handle non-finite values.
Results may differ from a plain program's by a relative error of at most 0.02.
Values may be sent and summed in bfloat16 or wider, within the bound.
A program may use at most 192 MiB of HBM per device.

v0:
```python
import jax
import jax.numpy as jnp
from jax import lax
from jax.sharding import PartitionSpec as P

HEAD_DIM = 128
BLOCK = 256


def prefix(array, axis, combine, identity, reverse):
    length, place = (lax.axis_size(axis), lax.axis_index(axis))
    everything = jax.tree.map(
        lambda part, kind: lax.all_gather(part.astype(kind), axis),
        array,
        (jnp.bfloat16, jnp.bfloat16),
    )
    start = jax.tree.map(
        lambda part, zero: jnp.broadcast_to(jnp.asarray(zero, part.dtype), part.shape),
        array,
        identity,
    )

    def turn(k, before):
        at = length - 1 - k if reverse else k
        reached = at > place if reverse else at < place
        new = combine(
            before, jax.tree.map(lambda part, own: part[at].astype(own.dtype), everything, array)
        )
        return jax.tree.map(lambda a, b: jnp.where(reached, a, b), new, before)

    return lax.fori_loop(0, length, turn, start)


def silu_slope(point):
    sigma = jax.nn.sigmoid(point)
    return sigma * (1.0 + point * (1.0 - sigma))


def block_factors(decay_sum, doc_index, doc_begin):
    inside = jnp.arange(doc_index.shape[-1], dtype=jnp.int32)
    causal = inside[:, None] >= inside[None, :]
    same_doc = (doc_index[:, :, None] == doc_index[:, None, :]) & causal[None]
    spread = jnp.minimum(decay_sum[..., :, None] - decay_sum[..., None, :], 0.0)
    pair_weight = jnp.where(same_doc[None], jnp.exp(spread), 0.0)
    to_end = jnp.where(
        (doc_index == doc_index[:, -1:])[None], jnp.exp(decay_sum[..., -1:] - decay_sum), 0.0
    )
    began_flag = doc_index == doc_index[:, :1] - doc_begin[:, :1]
    from_start = jnp.where(began_flag[None], jnp.exp(decay_sum), 0.0)
    return (pair_weight, to_end, from_start, from_start[..., -1])


def combine_states(earlier, later):
    return (earlier[0] * later[0], later[0][:, None, None] * earlier[1] + later[1])


def body(inputs, projection, cotangent, log_decay, document_starts):
    tokens = inputs.shape[0]
    heads_here = log_decay.shape[0]
    local_cols = cotangent.shape[1]
    blocks = tokens // BLOCK
    query_scale = HEAD_DIM ** (-0.5)
    features = lax.all_gather(inputs, "head", axis=1, tiled=True)
    weights_all = lax.all_gather(projection, "seq", axis=0, tiled=True)
    projected = jnp.einsum("td,dkc->tkc", features, weights_all, preferred_element_type=jnp.float32)
    queries = (jax.nn.silu(projected[:, 0]) * query_scale).astype(jnp.bfloat16)
    keys = jax.nn.silu(projected[:, 1]).astype(jnp.bfloat16)
    values = projected[:, 2].astype(jnp.bfloat16)

    def split_blocks(table):
        return table.reshape(blocks, BLOCK, heads_here, HEAD_DIM).transpose(2, 0, 1, 3)

    def merge_blocks(table):
        return table.transpose(1, 2, 0, 3).reshape(tokens, local_cols)

    queries_b = split_blocks(queries)
    keys_b = split_blocks(keys)
    values_b = split_blocks(values)
    upstream = split_blocks(cotangent)
    offset = lax.axis_index("seq") * tokens
    positions = offset + jnp.arange(tokens, dtype=jnp.int32)
    doc_index = (
        jnp.sum((document_starts[None, :] <= positions[:, None]).astype(jnp.int32), axis=1) - 1
    )
    doc_begin = jnp.any(document_starts[None, :] == positions[:, None], axis=1).astype(jnp.int32)
    decay_sum = jnp.cumsum(log_decay.reshape(heads_here, blocks, BLOCK), axis=-1)
    pair_weight, to_end, from_start, block_decay = block_factors(
        decay_sum, doc_index.reshape(blocks, BLOCK), doc_begin.reshape(blocks, BLOCK)
    )
    keys_weighted = (keys_b.astype(jnp.float32) * to_end[..., None]).astype(jnp.bfloat16)
    queries_weighted = (queries_b.astype(jnp.float32) * from_start[..., None]).astype(jnp.bfloat16)
    key_state = jnp.einsum(
        "hbse,hbsf->hbef", keys_weighted, values_b, preferred_element_type=jnp.float32
    )
    query_state = jnp.einsum(
        "hbte,hbtf->hbef", queries_weighted, upstream, preferred_element_type=jnp.float32
    )

    def local_step(carry, item):
        return (combine_states(carry, item), carry)

    ones = jnp.ones((heads_here,), jnp.float32)
    empty = jnp.zeros((heads_here, HEAD_DIM, HEAD_DIM), jnp.float32)
    (device_decay, device_keys), (prior_decay, prior_keys) = lax.scan(
        local_step, (ones, empty), (block_decay.T, key_state.swapaxes(0, 1))
    )
    (device_decay_back, device_query), (later_decay, later_query) = lax.scan(
        local_step, (ones, empty), (block_decay.T, query_state.swapaxes(0, 1)), reverse=True
    )
    forward_in = prefix((device_decay, device_keys), "seq", combine_states, (ones, empty), False)[1]
    backward_in = prefix(
        (device_decay_back, device_query), "seq", combine_states, (ones, empty), True
    )[1]
    state_before = (
        (prior_decay[:, :, None, None] * forward_in[None] + prior_keys)
        .swapaxes(0, 1)
        .astype(jnp.bfloat16)
    )
    state_after = (
        (later_decay[:, :, None, None] * backward_in[None] + later_query)
        .swapaxes(0, 1)
        .astype(jnp.bfloat16)
    )
    query_key = (
        jnp.einsum("hbte,hbse->hbts", queries_b, keys_b, preferred_element_type=jnp.float32)
        * pair_weight
    ).astype(jnp.bfloat16)
    value_score = (
        jnp.einsum("hbtf,hbsf->hbts", upstream, values_b, preferred_element_type=jnp.float32)
        * pair_weight
    ).astype(jnp.bfloat16)
    query_gradient = jnp.einsum(
        "hbts,hbse->hbte", value_score, keys_b, preferred_element_type=jnp.float32
    ) + from_start[..., None] * jnp.einsum(
        "hbtf,hbef->hbte", upstream, state_before, preferred_element_type=jnp.float32
    )
    key_gradient = jnp.einsum(
        "hbts,hbte->hbse", value_score, queries_b, preferred_element_type=jnp.float32
    ) + to_end[..., None] * jnp.einsum(
        "hbsf,hbef->hbse", values_b, state_after, preferred_element_type=jnp.float32
    )
    value_gradient = jnp.einsum(
        "hbts,hbtf->hbsf", query_key, upstream, preferred_element_type=jnp.float32
    ) + to_end[..., None] * jnp.einsum(
        "hbse,hbef->hbsf", keys_b, state_after, preferred_element_type=jnp.float32
    )
    project_gradient = jnp.stack(
        [
            merge_blocks(query_gradient) * silu_slope(projected[:, 0]) * query_scale,
            merge_blocks(key_gradient) * silu_slope(projected[:, 1]),
            merge_blocks(value_gradient),
        ],
        axis=1,
    ).astype(jnp.bfloat16)
    partial_value = jnp.einsum(
        "tkc,dkc->td", project_gradient, weights_all, preferred_element_type=jnp.float32
    )
    input_gradient = lax.psum_scatter(
        partial_value.astype(jnp.bfloat16), "head", scatter_dimension=1, tiled=True
    )
    weight_gradient = lax.psum_scatter(
        jnp.einsum(
            "td,tkc->dkc", features, project_gradient, preferred_element_type=jnp.float32
        ).astype(jnp.bfloat16),
        "seq",
        scatter_dimension=0,
        tiled=True,
    )
    return (input_gradient, weight_gradient)


def solution(mesh):
    placed = (P("seq", "head"), P("seq", None, "head"), P("seq", "head"), P("head", "seq"), P())
    return jax.shard_map(
        body,
        mesh=mesh,
        in_specs=placed,
        out_specs=(P("seq", "head"), P("seq", None, "head")),
        check_vma=False,
    )
```

profile of v0, /device:TPU:0, one launch (start us, length us, event | category | flops | bytes accessed | tf_op | source)
XLA Modules:
  0.0 778.4 jit_solution(1221711399798025846)
XLA Ops:
  8.8 4.8 reduce-window.6
  14.3 1.1 reshape.181
  19.3 109.7 %all-gather.7.cloned.1.call-done = bf16[1024,6144]{1,0:T(8,128)(2,1)} async-done(((bf16[1024,768]{1,0:T(8,128)(2,1)}), bf16[1024,6144]{1,0:T(8,128)(2,1)}) %all-gather.7.cloned.1.call-update) | async-done | bytes 12582928 | tf_op jit(solution)/shard_map/all_gather | solution.py:63
  129.1 175.4 %all-gather.9.cloned.1.call-done = bf16[6144,3,512]{2,0,1:T(8,128)(2,1)} async-done(((bf16[1536,3,512]{2,0,1:T(8,128)(2,1)}), bf16[6144,3,512]{2,0,1:T(8,128)(2,1)}) %all-gather.9.cloned.1.call-update) | async-done | bytes 18874384 | tf_op jit(solution)/shard_map/all_gather | solution.py:64
  304.5 23.7 %fusion.9 = f32[1024,3,512]{2,0,1:T(8,128)S(1)} fusion(bf16[6144,3,512]{2,0,1:T(8,128)(2,1)} %all-gather.9.cloned.1.call-done, bf16[1024,6144]{1,0:T(8,128)(2,1)} %all-gather.7.cloned.1.call-done), kind=kOutput, calls=%fused_computation.23 | convolution fusion | flops 19327352832 | bytes 37748736 | tf_op jit(solution)/shard_map/td,dkc->tkc/dot_general | solution.py:65
  328.2 2.0 fusion.57
  330.3 1.2 copy-done
  331.4 1.1 slice.68
  332.5 1.7 squeeze.57
  334.3 2.1 multiply_convert_fusion.6
  336.4 3.0 squeeze.59
  339.5 3.9 convolution_bitcast_fusion
  343.5 4.6 while.70
  343.6 1.1 bitcast_add_fusion.5
  344.7 1.1 bitcast_add_fusion.5
  345.9 1.1 bitcast_add_fusion.5
  347.0 1.1 bitcast_add_fusion.5
  349.1 1.3 convert_element_type.127
  350.4 5.5 fusion.16
  355.9 3.7 fusion.11
  359.7 2.4 convolution_bitcast_fusion.1
  362.1 1.1 broadcast.126.clone.1
  363.2 7.5 while.68
  363.9 1.0 bitcast_add_fusion.4
  365.7 1.0 bitcast_add_fusion.4
  367.6 1.0 bitcast_add_fusion.4
  369.4 1.0 bitcast_add_fusion.4
  370.7 4.5 fusion.20
  375.6 3.7 fusion.26
  379.3 8.9 %all-reduce.2 = (bf16[16]{0:T(256)(128)(2,1)S(1)}, bf16[16]{0:T(256)(128)(2,1)S(1)}) all-reduce(bf16[16]{0:T(256)(128)(2,1)S(1)} %dynamic-update-slice.1, bf16[16]{0:T(256)(128)(2,1)S(1)} %dynamic-update-slice), channel_id=4, replica_groups=mesh['seq'=4,'head'=8] {'seq'}, use_global_device_ids=true, to_apply=%add.1 | all-reduce | flops 32 | bytes 128
  388.3 11.3 %all-gather.3 = bf16[16,128,128]{2,1,0:T(8,128)(2,1)} all-gather(bf16[4,128,128]{2,1,0:T(8,128)(2,1)S(1)} %convert_element_type.142), channel_id=5, replica_groups=mesh['seq'=4,'head'=8] {'seq'}, dimensions={0}, use_global_device_ids=true | all-gather | bytes 655360 | tf_op jit(solution)/shard_map/all_gather | solution.py:13
  399.6 4.2 while.71
  403.8 2.4 fusion.13
  407.0 1.2 stack_reshape.4
  408.4 9.3 %all-gather.1 = bf16[16,128,128]{2,1,0:T(8,128)(2,1)S(1)} all-gather(bf16[4,128,128]{2,1,0:T(8,128)(2,1)S(1)} %convert_element_type.135), channel_id=3, replica_groups=mesh['seq'=4,'head'=8] {'seq'}, dimensions={0}, use_global_device_ids=true | all-gather | bytes 655360 | tf_op jit(solution)/shard_map/all_gather | solution.py:13
  418.3 2.7 fusion.15
  421.1 2.7 copy.160
  423.7 3.1 reshape.184
  426.9 2.0 fusion.14
  428.9 2.7 copy.169
  431.6 3.2 reshape.185
  434.8 4.4 multiply_convert_fusion.4
  440.2 28.6 %convert_bitcast_fusion = bf16[6144,3,512]{0,2,1:T(8,128)(2,1)} fusion(bf16[1024,6144]{1,0:T(8,128)(2,1)} %all-gather.7.cloned.1.call-done, bf16[1024,1,512]{2,0,1:T(8,128)(2,1)S(1)} %copy-done.9, bf16[1024,1,512]{2,0,1:T(8,128)(2,1)S(1)} %get-tuple-element.645, bf16[1024,1,512]{2,0,1:T(8,128)(2,1)S(1)} %get-tuple-element.644), kind=kOutput, calls=%fused_computation.21 | convolution fusion | flops 19339935744 | bytes 34603008 | tf_op jit(solution)/shard_map/td,tkc->dkc/dot_general | solution.py:162
  468.9 1.1 copy-done.7
  470.3 24.9 %bitcast_convert_fusion.2 = bf16[1024,6144]{1,0:T(8,128)(2,1)} fusion(bf16[6144,3,512]{2,0,1:T(8,128)(2,1)} %all-gather.9.cloned.1.call-done, bf16[1024,1,512]{2,0,1:T(8,128)(2,1)S(1)} %copy-done.10, bf16[1024,1,512]{2,0,1:T(8,128)(2,1)S(1)} %copy-done.7, bf16[1024,1,512]{2,0,1:T(8,128)(2,1)S(1)} %get-tuple-element.644), kind=kOutput, calls=%fused_computation.20 | convolution fusion | flops 19336790016 | bytes 34603008 | tf_op jit(solution)/shard_map/tkc,dkc->td/dot_general | solution.py:155
  495.3 144.5 %reduce-scatter.5.cloned.1.call-done = bf16[1536,3,512]{0,2,1:T(8,128)(2,1)} async-done(((bf16[6144,3,512]{0,2,1:T(8,128)(2,1)}), bf16[1536,3,512]{0,2,1:T(8,128)(2,1)}) %reduce-scatter.5.cloned.1.call-update) | async-done | bytes 4718608 | tf_op jit(solution)/shard_map/reduce_scatter | solution.py:161
  639.8 6.6 copy.174
  646.4 125.4 %reduce-scatter.3.cloned.1.call-done = bf16[1024,768]{1,0:T(8,128)(2,1)} async-done(((bf16[1024,6144]{1,0:T(8,128)(2,1)}), bf16[1024,768]{1,0:T(8,128)(2,1)}) %reduce-scatter.3.cloned.1.call-update) | async-done | bytes 1572880 | tf_op jit(solution)/shard_map/reduce_scatter | solution.py:158
  (125 shorter events, 17.8 us)
Async XLA Ops:
  7.2 121.9 %all-gather.7.cloned.1.call-start = ((), (), s32[]{:S(2)}) async-start(), calls=%async_computation.2 | async-start | bytes 14155776 | tf_op jit(solution)/shard_map/all_gather | solution.py:63
  7.9 0.9 copy-start.11
  7.9 6.2 copy-start.12
  7.9 6.3 copy-start.8
  7.9 296.5 %all-gather.9.cloned.1.call-start = ((), (), s32[]{:S(2)}) async-start(), calls=%async_computation.3 | async-start | bytes 23592960 | tf_op jit(solution)/shard_map/all_gather | solution.py:64
  8.7 631.1 %reduce-scatter.5.cloned.1.call-start = ((), (), s32[]{:S(2)}) async-start(), calls=%async_computation.5 | async-start | bytes 23592960 | tf_op jit(solution)/shard_map/reduce_scatter | solution.py:161
  15.4 2.4 copy-start.13
  328.2 3.2 copy-start
  336.4 3.0 copy-start.4
  348.1 1.0 copy-start.1
  408.4 10.0 %copy-start.5 = (bf16[4,256,4,128]{3,2,1,0:T(4,128)(2,1)S(1)}, bf16[4,256,4,128]{3,2,1,0:T(4,128)(2,1)}, u32[]{:S(2)}) copy-start(bf16[4,256,4,128]{3,2,1,0:T(4,128)(2,1)} %reshape.181) | copy-start | bytes 3145732
  423.7 3.1 copy-start.2
  431.6 3.2 copy-start.3
  434.8 5.4 copy-start.9
  439.3 1.0 copy-start.6
  468.8 1.2 copy-start.7
  468.8 1.5 copy-start.10
  468.8 303.0 %reduce-scatter.3.cloned.1.call-start = ((), (), s32[]{:S(2)}) async-start(), calls=%async_computation.4 | async-start | bytes 14155776 | tf_op jit(solution)/shard_map/reduce_scatter | solution.py:158
Sparse Core Ops, SparseCore 0:
  9.6 119.4 all-gather.6
  130.9 173.4 all-gather.8
  468.9 170.7 reduce-scatter.4
  642.6 129.1 reduce-scatter.2
where the time goes:
time: 779 us; the launch traced here: 778 us
  waiting for transfers between devices  557 us (72%)
  matrix products  108 us (14%)
  local copies, waits for them, and re-layouts  40 us (5%)
  blocking collectives  29.5 us (4%)
  other arithmetic  28.8 us (4%)
  between operations  14.8 us (2%)
    all_gather x1, waiting for transfers between devices, body(): weights_all = lax.all_gather(projection, 'seq', axis=0, tiled=True)  175 us
    reduce_scatter x1, waiting for transfers between devices, body(): lax.psum_scatter(jnp.einsum('td,tkc->dkc', features, project_gradient, pr...  145 us
    reduce_scatter x1, waiting for transfers between devices, body(): lax.psum_scatter(partial_value.astype(jnp.bfloat16), 'head', scatter_dime...  125 us
    all_gather x1, waiting for transfers between devices, body(): features = lax.all_gather(inputs, 'head', axis=1, tiled=True)  110 us
    dot_general x1, matrix products, body(): jnp.einsum('td,tkc->dkc', features, project_gradient, preferred_element_t...  28.6 us
    dot_general x1, matrix products, body(): jnp.einsum('tkc,dkc->td', project_gradient, weights_all, preferred_elemen...  24.9 us
    dot_general x1, matrix products, body(): jnp.einsum('td,dkc->tkc', features, weights_all, preferred_element_type=j...  23.7 us
    all_gather x2, blocking collectives, prefix(): lax.all_gather(part.astype(kind), axis)  20.6 us
  transfers between devices with their start and end apart: 4, of which 4 were waited for; matrix products, arithmetic and copies ran while one was open for 5% of the time, Pallas kernels for 0%

commit v1 on v0

--- a/solution.py
+++ b/solution.py
@@ -61,7 +61,21 @@
     blocks = tokens // BLOCK
     query_scale = HEAD_DIM ** (-0.5)
     features = lax.all_gather(inputs, "head", axis=1, tiled=True)
-    weights_all = lax.all_gather(projection, "seq", axis=0, tiled=True)
+    ways, here, step = (lax.axis_size("seq"), lax.axis_index("seq"), projection.shape[0])
+    dims = [n * ways if d == 0 else n for d, n in enumerate(projection.shape)]
+    full = lax.dynamic_update_slice_in_dim(
+        jnp.zeros(dims, projection.dtype), projection, here * step, axis=0
+    )
+    going_up = going_down = projection
+    for far in range(1, ways // 2 + 1):
+        going_up = lax.ppermute(going_up, "seq", [(d, (d + 1) % ways) for d in range(ways)])
+        full = lax.dynamic_update_slice_in_dim(full, going_up, (here - far) % ways * step, axis=0)
+        if 2 * far < ways:
+            going_down = lax.ppermute(going_down, "seq", [(d, (d - 1) % ways) for d in range(ways)])
+            full = lax.dynamic_update_slice_in_dim(
+                full, going_down, (here + far) % ways * step, axis=0
+            )
+    weights_all = full
     projected = jnp.einsum("td,dkc->tkc", features, weights_all, preferred_element_type=jnp.float32)
     queries = (jax.nn.silu(projected[:, 0]) * query_scale).astype(jnp.bfloat16)
     keys = jax.nn.silu(projected[:, 1]).astype(jnp.bfloat16)

time: 779 us -> 824 us (1.058); the launches traced: 778 us -> 814 us
  local copies, waits for them, and re-layouts: 40 us -> 77.2 us
  waiting for transfers between devices: 557 us -> 542 us
    ppermute x0 -> x3, waiting for transfers between devices: none -> 272 us  [the longest x2 198 us: body(): lax.ppermute(going_up, 'seq', [(d, (d + 1) % ways) for d in range(ways)])]
    all_gather x1 -> x0, waiting for transfers between devices: 175 us -> none  [body(): weights_all = lax.all_gather(projection, 'seq', axis=0, tiled=True)]
    all_gather x1, waiting for transfers between devices: 110 us -> 0.01 us  [body(): features = lax.all_gather(inputs, 'head', axis=1, tiled=True)]
    dynamic_update_slice x0 -> x4, local copies, waits for them, and re-layouts: none -> 17 us  [the longest x2 9.63 us: body(): lax.dynamic_update_slice_in_dim(full, going_up, (here - far) % ways * ste...]
  transfers between devices with their start and end apart: 4 -> 6, of which waited for: 4 -> 5; matrix products, arithmetic and copies ran while one was open for 5% -> 8% of each run, Pallas kernels for 0% -> 0%
where the time goes in v1:
time: 824 us; the launch traced here: 814 us
  waiting for transfers between devices  542 us (66%)
  matrix products  111 us (13%)
  local copies, waits for them, and re-layouts  77.2 us (9%)
  other arithmetic  33 us (4%)
  blocking collectives  29.8 us (4%)
  between operations  15 us (2%)
    ppermute x2, waiting for transfers between devices, body(): lax.ppermute(going_up, 'seq', [(d, (d + 1) % ways) for d in range(ways)])  198 us
    reduce_scatter x1, waiting for transfers between devices, body(): lax.psum_scatter(jnp.einsum('td,tkc->dkc', features, project_gradient, pr...  144 us
    reduce_scatter x1, waiting for transfers between devices, body(): lax.psum_scatter(partial_value.astype(jnp.bfloat16), 'head', scatter_dime...  126 us
    ppermute x1, waiting for transfers between devices, body(): lax.ppermute(going_down, 'seq', [(d, (d - 1) % ways) for d in range(ways)])  74 us
    dot_general x1, matrix products, body(): jnp.einsum('td,tkc->dkc', features, project_gradient, preferred_element_t...  27.9 us
    dot_general x1, matrix products, body(): jnp.einsum('tkc,dkc->td', project_gradient, weights_all, preferred_elemen...  25.5 us
    dot_general x1, matrix products, body(): jnp.einsum('td,dkc->tkc', features, weights_all, preferred_element_type=j...  23.9 us
    all_gather x2, blocking collectives, prefix(): lax.all_gather(part.astype(kind), axis)  20.7 us
  transfers between devices with their start and end apart: 6, of which 5 were waited for; matrix products, arithmetic and copies ran while one was open for 8% of the time, Pallas kernels for 0%

profile of v1, /device:TPU:0, one launch (start us, length us, event | category | flops | bytes accessed | tf_op | source)
XLA Modules:
  0.0 814.1 jit_solution(1649570588284470685)
XLA Ops:
  8.0 3.0 collective-permute-start
  12.0 102.9 %collective-permute-done = bf16[1536,3,512]{2,0,1:T(8,128)(2,1)} collective-permute-done((bf16[1536,3,512]{2,0,1:T(8,128)(2,1)}, bf16[1536,3,512]{2,0,1:T(8,128)(2,1)}, u32[]{:S(2)}, u32[]{:S(2)}) %collective-permute-start) | collective-permute-done | bytes 4718624 | tf_op jit(solution)/shard_map/ppermute | solution.py:71
  116.7 4.8 reduce-window.6
  127.9 7.2 broadcast_in_dim.89
  135.1 2.6 constant_dynamic-update-slice_fusion.3
  137.7 4.8 constant_dynamic-update-slice_fusion.2
  142.5 74.0 %collective-permute-done.1 = bf16[1536,3,512]{2,0,1:T(8,128)(2,1)} collective-permute-done((bf16[1536,3,512]{2,0,1:T(8,128)(2,1)}, bf16[1536,3,512]{2,0,1:T(8,128)(2,1)}, u32[]{:S(2)}, u32[]{:S(2)}) %collective-permute-start.1) | collective-permute-done | bytes 4718624 | tf_op jit(solution)/shard_map/ppermute | solution.py:74
  216.5 4.8 constant_dynamic-update-slice_fusion.1
  221.3 95.0 %collective-permute-done.2 = bf16[1536,3,512]{2,0,1:T(8,128)(2,1)} collective-permute-done((bf16[1536,3,512]{2,0,1:T(8,128)(2,1)}, bf16[1536,3,512]{2,0,1:T(8,128)(2,1)}, u32[]{:S(2)}, u32[]{:S(2)}) %collective-permute-start.2) | collective-permute-done | bytes 4718624 | tf_op jit(solution)/shard_map/ppermute | solution.py:71
  316.3 4.8 constant_dynamic-update-slice_fusion
  321.1 23.9 %fusion.12 = f32[1024,3,512]{0,2,1:T(8,128)S(1)} fusion(bf16[6144,3,512]{2,0,1:T(8,128)(2,1)} %constant_dynamic-update-slice_fusion, bf16[1024,6144]{1,0:T(8,128)(2,1)} %all-gather.6.cloned.1.call-done), kind=kOutput, calls=%fused_computation.30 | convolution fusion | flops 19327352832 | bytes 37748736 | tf_op jit(solution)/shard_map/td,dkc->tkc/dot_general | solution.py:79
  345.1 2.9 fusion.57
  348.9 1.2 slice.68
  350.1 2.2 squeeze.57
  352.4 1.9 copy.151
  354.2 2.1 multiply_convert_fusion.6
  356.4 3.2 squeeze.59
  359.6 3.4 copy.167
  363.0 4.0 convolution_bitcast_fusion
  367.1 4.6 while.70
  372.7 2.6 convert_element_type.127
  375.4 1.8 copy.146
  377.1 5.5 fusion.19
  382.6 3.8 fusion.11
  386.4 2.4 convolution_bitcast_fusion.1
  389.9 7.3 while.68
  397.2 4.4 fusion.23
  402.1 3.7 fusion.29
  405.7 9.1 %all-reduce.2 = (bf16[16]{0:T(256)(128)(2,1)S(1)}, bf16[16]{0:T(256)(128)(2,1)S(1)}) all-reduce(bf16[16]{0:T(256)(128)(2,1)S(1)} %dynamic-update-slice.1, bf16[16]{0:T(256)(128)(2,1)S(1)} %dynamic-update-slice), channel_id=4, replica_groups=mesh['seq'=4,'head'=8] {'seq'}, use_global_device_ids=true, to_apply=%add.1 | all-reduce | flops 32 | bytes 128
  415.0 10.5 %all-gather.3 = bf16[16,128,128]{2,1,0:T(8,128)(2,1)} all-gather(bf16[4,128,128]{2,1,0:T(8,128)(2,1)S(1)} %convert_element_type.142), channel_id=5, replica_groups=mesh['seq'=4,'head'=8] {'seq'}, dimensions={0}, use_global_device_ids=true | all-gather | bytes 655360 | tf_op jit(solution)/shard_map/all_gather | solution.py:13
  425.5 4.2 while.71
  429.7 3.2 fusion.16
  432.9 1.7 copy.177
  434.6 1.5 stack_reshape.4
  436.2 10.2 %all-gather.1 = bf16[16,128,128]{2,1,0:T(8,128)(2,1)} all-gather(bf16[4,128,128]{2,1,0:T(8,128)(2,1)S(1)} %convert_element_type.135), channel_id=3, replica_groups=mesh['seq'=4,'head'=8] {'seq'}, dimensions={0}, use_global_device_ids=true | all-gather | bytes 655360 | tf_op jit(solution)/shard_map/all_gather | solution.py:13
  446.4 4.4 while.69
  450.8 3.7 fusion.18
  454.5 2.9 copy.165
  457.4 3.4 reshape.184
  460.8 3.0 fusion.17
  463.8 2.9 copy.174
  466.7 3.4 reshape.185
  470.2 4.4 multiply_convert_fusion.4
  475.9 27.9 %convert_bitcast_fusion = bf16[6144,3,512]{0,2,1:T(8,128)(2,1)} fusion(bf16[1024,6144]{1,0:T(8,128)(2,1)} %all-gather.6.cloned.1.call-done, bf16[1024,1,512]{0,2,1:T(8,128)(2,1)S(1)} %copy-done.11, bf16[1024,1,512]{0,2,1:T(8,128)(2,1)S(1)} %get-tuple-element.645, bf16[1024,1,512]{0,2,1:T(8,128)(2,1)S(1)} %get-tuple-element.644), kind=kOutput, calls=%fused_computation.21 | convolution fusion | flops 19339935744 | bytes 34603008 | tf_op jit(solution)/shard_map/td,tkc->dkc/dot_general | solution.py:176
  505.4 25.5 %bitcast_convert_fusion.2 = bf16[1024,6144]{1,0:T(8,128)(2,1)} fusion(bf16[6144,3,512]{2,0,1:T(8,128)(2,1)} %constant_dynamic-update-slice_fusion, bf16[1024,1,512]{0,2,1:T(8,128)(2,1)} %stack_reshape.4, bf16[1024,1,512]{0,2,1:T(8,128)(2,1)S(1)} %copy-done.9, bf16[1024,1,512]{0,2,1:T(8,128)(2,1)S(1)} %copy-done.7), kind=kOutput, calls=%fused_computation.20 | convolution fusion | flops 19336790016 | bytes 34603008 | tf_op jit(solution)/shard_map/tkc,dkc->td/dot_general | solution.py:169
  530.9 144.3 %reduce-scatter.5.cloned.1.call-done = bf16[1536,3,512]{0,2,1:T(8,128)(2,1)} async-done(((bf16[6144,3,512]{0,2,1:T(8,128)(2,1)}), bf16[1536,3,512]{0,2,1:T(8,128)(2,1)}) %reduce-scatter.5.cloned.1.call-update) | async-done | bytes 4718608 | tf_op jit(solution)/shard_map/reduce_scatter | solution.py:175
  675.2 6.6 copy.179
  681.8 125.6 %reduce-scatter.3.cloned.1.call-done = bf16[1024,768]{1,0:T(8,128)(2,1)} async-done(((bf16[1024,6144]{1,0:T(8,128)(2,1)}), bf16[1024,768]{1,0:T(8,128)(2,1)}) %reduce-scatter.3.cloned.1.call-update) | async-done | bytes 1572880 | tf_op jit(solution)/shard_map/reduce_scatter | solution.py:172
  (141 shorter events, 35.8 us)
Async XLA Ops:
  7.2 117.0 %copy-start.12 = (s32[4]{0:T(128)S(1)}, s32[4]{0:T(128)}, u32[]{:S(2)}) copy-start(s32[4]{0:T(128)} %param.17) | copy-start | bytes 52
  7.2 115.6 %copy-start.10 = (bf16[1024,512]{1,0:T(8,128)(2,1)S(1)}, bf16[1024,512]{1,0:T(8,128)(2,1)}, u32[]{:S(2)}) copy-start(bf16[1024,512]{1,0:T(8,128)(2,1)} %param.15) | copy-start | bytes 3145732
  7.2 313.9 %all-gather.6.cloned.1.call-start = ((), (), s32[]{:S(2)}) async-start(), calls=%async_computation.2 | async-start | bytes 14155776 | tf_op jit(solution)/shard_map/all_gather | solution.py:63
  7.9 667.2 %reduce-scatter.5.cloned.1.call-start = ((), (), s32[]{:S(2)}) async-start(), calls=%async_computation.4 | async-start | bytes 23592960 | tf_op jit(solution)/shard_map/reduce_scatter | solution.py:175
  8.0 106.9 %collective-permute-start = (bf16[1536,3,512]{2,0,1:T(8,128)(2,1)}, bf16[1536,3,512]{2,0,1:T(8,128)(2,1)}, u32[]{:S(2)}, u32[]{:S(2)}) collective-permute-start(bf16[1536,3,512]{2,0,1:T(8,128)(2,1)} %param.14), channel_id=1, source_target_pairs={{0,8},{8,16},{16,24},{24,0},{1,9},{9,17},{17,25},{25,1},{2,10},{10... | collective-permute-start | bytes 14155784 | tf_op jit(solution)/shard_map/ppermute | solution.py:71
  11.0 205.6 %collective-permute-start.1 = (bf16[1536,3,512]{2,0,1:T(8,128)(2,1)}, bf16[1536,3,512]{2,0,1:T(8,128)(2,1)}, u32[]{:S(2)}, u32[]{:S(2)}) collective-permute-start(bf16[1536,3,512]{2,0,1:T(8,128)(2,1)} %param.14), channel_id=1, source_target_pairs={{0,24},{8,0},{16,8},{24,16},{1,25},{9,1},{17,9},{25,17},{2,26},{10... | collective-permute-start | bytes 14155784 | tf_op jit(solution)/shard_map/ppermute | solution.py:74
  114.9 201.4 %collective-permute-start.2 = (bf16[1536,3,512]{2,0,1:T(8,128)(2,1)}, bf16[1536,3,512]{2,0,1:T(8,128)(2,1)}, u32[]{:S(2)}, u32[]{:S(2)}) collective-permute-start(bf16[1536,3,512]{2,0,1:T(8,128)(2,1)} %collective-permute-done), channel_id=1, source_target_pairs={{0,8},{8,16},{16,24},{24,0},{1,9},{9,17},{17,25},{25,1},{2,10},{10... | collective-permute-start | bytes 14155784 | tf_op jit(solution)/shard_map/ppermute | solution.py:71
  124.2 2.2 copy-start.13
  127.6 7.5 slice-start
  127.9 7.3 slice-start.1
  345.0 3.9 copy-start
  359.6 3.4 copy-start.4
  371.7 1.0 copy-start.1
  436.2 14.6 %copy-start.5 = (bf16[4,256,4,128]{3,2,1,0:T(4,128)(2,1)S(1)}, bf16[4,256,4,128]{3,2,1,0:T(4,128)(2,1)}, u32[]{:S(2)}) copy-start(bf16[4,256,4,128]{3,2,1,0:T(4,128)(2,1)} %reshape.181) | copy-start | bytes 3145732
  457.4 3.4 copy-start.2
  466.7 3.4 copy-start.3
  470.2 5.8 copy-start.11
  474.6 1.0 copy-start.6
  474.6 1.3 copy-start.8
  503.9 1.2 copy-start.7
  503.9 1.5 copy-start.9
  503.9 303.5 %reduce-scatter.3.cloned.1.call-start = ((), (), s32[]{:S(2)}) async-start(), calls=%async_computation.3 | async-start | bytes 14155776 | tf_op jit(solution)/shard_map/reduce_scatter | solution.py:172
Sparse Core Ops, SparseCore 0:
  9.6 119.4 all-gather.5
  504.0 171.1 reduce-scatter.4
  678.2 129.1 reduce-scatter.2
